TPU v7x, 32 devices: a whole 2x2x4 slice. The times are simulated.
32 devices in a mesh: gx: 4 (over y, x), gy: 4 (over z), gz: 2 (over core).
Axes of the slice: x: 2, y: 2, z: 4, core: 2. Of those that a mesh axis runs over, the one named last changes fastest.
Arguments:
- node_positions: float32 [3, 32, 32, 512], P(None, 'gx', 'gy', 'gz'), may hold values from 0 to 4, as said below
- control_positions: float32 [3, 65536], P(None, ('gx', 'gy', 'gz')), may hold values from 0 to 4, as said below
- control_coefficient_values: float32 [3, 65536], P(None, ('gx', 'gy', 'gz')), may hold values from -2.4 to 2.4
- support_pairs: int32 [4096, 3], P(('gx', 'gy', 'gz')), may hold values from 0 to 31, as said below
- live_counts: int32 [32], P(('gx', 'gy', 'gz')), may hold values from 32 to 128
- sliver_flags: int32 [32, 32, 512], P('gx', 'gy', 'gz'), may hold values 0 or 1
Outputs:
- displacement: float32 [3, 32, 32, 512], P(None, 'gx', 'gy', 'gz')
Inputs may be any that keep to these rules, and one draw needn't show every extreme that they name: `node_positions`: node coordinates lie within their node's cell of width 1 / 8, 1 / 8, 1 / 256 around the cell centre. `control_positions`: the control points of block o lie in the unit cube of that block. `support_pairs`: column 0 is a node tile below 32; column 1 is a block that differs from the row's own block by at most one along each of the three directions; column 2 is a slot below 4; slot p < 32 of every block names node tile p and the block itself.
All inputs are finite; a program needn't handle non-finite values. No bound on the sum of `sliver_flags` on one device may be relied on, other than what follows from the above.
Results may differ from a plain program's by a relative error of at most 0.0003.
Values sent between devices are 32-bit elements; how exact they have to be, the bound alone decides.
A program may use at most 64 MiB of HBM per device.

v0:
```python
import functools

import jax
import jax.numpy as jnp
from jax import lax
from jax.experimental import pallas as pl
from jax.experimental.pallas import tpu as pltpu
from jax.sharding import PartitionSpec as P

TILE = 512
CT = 4
PAIRS = 128
SWEEPS = 2
RADIUS = 1.5
OMEGA = 0.7
GROUP = 4
HALF = 256
bf16, f32 = jnp.bfloat16, jnp.float32


def split3(x):
    a = x.astype(bf16).astype(f32)
    r = x - a
    b = r.astype(bf16).astype(f32)
    return a, b, r - b


def row_ids():
    return lax.broadcasted_iota(jnp.int32, (8, TILE), 0)


def node_features(x_ref, t, origin):
    per = TILE // x_ref.shape[2]
    rows = row_ids()
    coords = []
    for c in range(3):
        row = jnp.concatenate(
            [x_ref[c, pl.ds(t * per + j, 1), :] for j in range(per)], axis=1
        )
        coords.append((row - origin[c]) * (1.0 / RADIUS))
    norm = coords[0] * coords[0] + coords[1] * coords[1] + coords[2] * coords[2]
    block = jnp.where(rows == 4, 1.0, 0.0)
    for i, row in enumerate(coords + [norm]):
        block = jnp.where(rows == i, jnp.broadcast_to(row, (8, TILE)), block)
    a, b, c = split3(block)
    return jnp.concatenate([a, a, b, b, a, c], 0).astype(bf16)


def control_features(raw, origin):
    rows = row_ids()
    shift = jnp.where(rows == 0, origin[0], jnp.where(rows == 1, origin[1], origin[2]))
    pos = jnp.where(rows < 3, (raw - shift) * (1.0 / RADIUS), 0.0)
    norm = jnp.sum(pos * pos, axis=0, keepdims=True)
    block = jnp.where(rows == 3, 1.0, -2.0 * pos)
    block = jnp.where(rows == 4, jnp.broadcast_to(norm, (8, TILE)), block)
    a, b, c = split3(block)
    return jnp.transpose(jnp.concatenate([a, b, a, b, c, a], 0)).astype(bf16)


def pair_sum(nodes, raw, origin):
    controls = control_features(raw, origin)
    high = raw.astype(bf16).astype(f32)
    coefs = jnp.concatenate([high, raw - high], 0).astype(bf16)
    coefs = jnp.concatenate([coefs, coefs], 1)
    sums = []
    for n in range(0, TILE, HALF):
        dist_sq = jnp.dot(controls, nodes[:, n : n + HALF], preferred_element_type=f32)
        dist_sq = jnp.minimum(jnp.maximum(dist_sq, 1e-20), 1.0)
        scaled = dist_sq * lax.rsqrt(dist_sq)
        fall = 1.0 - scaled
        fall2 = fall * fall
        weight = (fall2 * fall2) * (0.25 + scaled)
        top = weight.astype(bf16)
        rest = (weight - top.astype(f32)).astype(bf16)
        sums.append(
            jnp.dot(coefs, jnp.concatenate([top, rest], 0), preferred_element_type=f32)
        )
    return jnp.concatenate(sums, 1)


def peers(axis, shifts, wrap):
    count, me = lax.axis_size(axis), lax.axis_index(axis)
    for i, d in enumerate(shifts):
        if d == 0:
            continue
        step = d if wrap or d == 1 else d - count
        ahead = None if wrap else jnp.logical_and(me + step >= 0, me + step < count)
        behind = None if wrap else jnp.logical_and(me - step >= 0, me - step < count)
        yield i, (me + step + count) % count, (me - step + count) % count, ahead, behind


def when(cond, do):
    if cond is None:
        do()
    else:
        pl.when(cond)(do)


def gather_kernel(axes, half, slot_ref, live_ref, x_ref, pos_ref, coef_ref, pairs_ref, o_ref, table, x_both, mate_meta, own_ref, meta_ref, send, recv, extra, local):
    origin = [lax.axis_index(axis).astype(f32) + 0.5 for axis, _, _ in axes]
    for s in range(CT):
        own_ref[s, 0:3] = pos_ref[:, s * TILE : (s + 1) * TILE]
        own_ref[s, 3:6] = coef_ref[:, s * TILE : (s + 1) * TILE]
        own_ref[s, 6:8] = jnp.zeros((2, TILE), f32)
    meta_ref[0:3] = pairs_ref[...]
    meta_ref[3:8] = jnp.full((5, meta_ref.shape[1]), live_ref[0], jnp.int32)
    barrier = pltpu.get_barrier_semaphore()
    expected = 0
    for axis, shifts, wrap in axes:
        for _, ahead, _, there, _ in peers(axis, shifts, wrap):
            when(there, lambda axis=axis, ahead=ahead: pl.semaphore_signal(
                barrier, inc=1, device_id={axis: ahead}, device_id_type=pl.DeviceIdType.MESH))
            expected = expected + (1 if there is None else there.astype(jnp.int32))
    pl.semaphore_wait(barrier, expected)

    def views(k, i):
        if k == 0:
            return own_ref, table.at[0, 0, i]
        if k == 1:
            return table.at[0, 0], table.at[0, i]
        return table.at[0], table.at[i]

    def copies(k):
        axis, shifts, wrap = axes[k]
        for i, ahead, behind, has_ahead, has_behind in peers(axis, shifts, wrap):
            src, dst = views(k, i)
            copy = pltpu.make_async_remote_copy(
                src_ref=src, dst_ref=dst, send_sem=send.at[k, i], recv_sem=recv.at[k, i],
                device_id={axis: behind}, device_id_type=pl.DeviceIdType.MESH)
            yield copy, has_behind, has_ahead

    def start(k):
        for copy, goes, _ in copies(k):
            when(goes, copy.start)

    def land(k):
        for copy, goes, comes in copies(k):
            when(comes, copy.wait_recv)
            when(goes, copy.wait_send)

    gx_name = axes[0][0]
    count = lax.axis_size(gx_name)
    mate = (lax.axis_index(gx_name) + half) % count
    keep = [
        pltpu.make_async_copy(own_ref, table.at[0, 0, 0], local.at[0]),
        pltpu.make_async_copy(x_ref, x_both.at[1], local.at[1]),
    ]
    for copy in keep:
        copy.start()
    start(0)
    swaps = [
        pltpu.make_async_remote_copy(
            src_ref=src, dst_ref=dst, send_sem=extra.at[0, n], recv_sem=extra.at[1, n],
            device_id={gx_name: mate}, device_id_type=pl.DeviceIdType.MESH)
        for n, (src, dst) in enumerate(((meta_ref, mate_meta), (x_ref, x_both.at[0])))
    ]
    swaps[0].start()

    groups = o_ref.shape[0] // GROUP

    def compute(low, high):
        @pl.loop(low, high)
        def _(g):
            for j in range(GROUP):
                i = g * GROUP + j
                nodes = node_features(x_ref, i, origin)
                o_ref[i] = pair_sum(nodes, own_ref[slot_ref[2, i]], origin)

    cuts = [0, groups // 4, groups // 4 * 3, groups]
    for k in range(3):
        compute(cuts[k], cuts[k + 1])
        if k == 0:
            for copy in keep:
                copy.wait()
        land(k)
        if k < 2:
            start(k + 1)
        if k == 0:
            swaps[1].start()
    for copy in swaps:
        copy.wait()


def finish(acc, at, o_ref):
    per = TILE // o_ref.shape[2]
    width = o_ref.shape[2]
    for t in range(o_ref.shape[1] // per):
        both = 4.0 * (acc[at + t, :8] + acc[at + t, 8:])
        for j in range(per):
            o_ref[:, t * per + j, :] = both[3:6, j * width : (j + 1) * width]


def rest_kernel(axes, half, meta, live, mate_meta, x_both, table, init, sent_ref, o_ref, acc):
    ntiles = init.shape[0]
    trash = 2 * ntiles
    acc[:ntiles] = jnp.zeros_like(init)
    acc[ntiles:trash] = init[...]
    here = [lax.axis_index(axis) for axis, _, _ in axes]
    counts = [lax.axis_size(axis) for axis, _, _ in axes]
    mate_at = lax.rem(here[0] + half, counts[0])
    mine, theirs = live[0], mate_meta[3, 0]
    goal = lax.div(mine + theirs + 1, 2)
    skip = jnp.minimum(goal, theirs)
    helped = theirs - skip
    total = helped + jnp.minimum(mine, goal) - ntiles

    def source(owner, slot):
        owners = (
            lax.div(owner, counts[1] * counts[2]),
            lax.rem(lax.div(owner, counts[2]), counts[1]),
            lax.rem(owner, counts[2]),
        )
        at = 0
        for k in (2, 1, 0):
            shifts = axes[k][1]
            rel = lax.rem(owners[k] - here[k] + counts[k], counts[k])
            at = at * len(shifts) + sum(jnp.where(rel == d, i, 0) for i, d in enumerate(shifts))
        return at * CT + slot

    @pl.loop(0, lax.div(total + GROUP - 1, GROUP))
    def _(g):
        for j in range(GROUP):
            p = g * GROUP + j
            for_mate = p < helped
            slot = jnp.minimum(jnp.where(for_mate, skip + p, ntiles + p - helped), PAIRS - 1)
            t, owner, tile = (
                jnp.where(for_mate, mate_meta[c, slot], meta[c, slot]) for c in range(3)
            )
            part = jnp.where(for_mate, 0, 1)
            origin = [
                jnp.where(for_mate, mate_at, here[0]).astype(f32) + 0.5,
                here[1].astype(f32) + 0.5,
                here[2].astype(f32) + 0.5,
            ]
            nodes = node_features(x_both.at[part], t, origin)
            into = jnp.where(p < total, part * ntiles + t, trash)
            acc[into] += pair_sum(nodes, table[source(owner, tile)], origin)

    finish(acc, 0, sent_ref)
    finish(acc, ntiles, o_ref)


def smooth_kernel(half, sent_ref, mine_ref, flag_ref, o_ref, back, m, yface, xh, yh, zh, sems, zsend):
    names = ("gx", "gy", "gz")
    here = [lax.axis_index(a) for a in names]
    counts = [lax.axis_size(a) for a in names]
    mate = (here[0] + half) % counts[0]
    mesh_id = pl.DeviceIdType.MESH
    barrier = pltpu.get_barrier_semaphore()
    pl.semaphore_signal(barrier, inc=1, device_id={"gx": mate}, device_id_type=mesh_id)
    expected = 1
    faces = []
    for k, axis in enumerate(names):
        for side, step in enumerate((-1, 1)):
            at = here[k] + step
            there = jnp.logical_and(at >= 0, at < counts[k])
            at = jnp.clip(at, 0, counts[k] - 1)
            faces.append((k, side, axis, at, there))
            pl.when(there)(lambda axis=axis, at=at: pl.semaphore_signal(
                barrier, inc=1, device_id={axis: at}, device_id_type=mesh_id))
            expected = expected + there.astype(jnp.int32)
    pl.semaphore_wait(barrier, expected)
    swap = pltpu.make_async_remote_copy(
        src_ref=sent_ref, dst_ref=back, send_sem=sems.at[0, 2, 0, 0], recv_sem=sems.at[0, 2, 1, 0],
        device_id={"gx": mate}, device_id_type=mesh_id)
    swap.start()
    halos = (xh, yh, zh)
    for k, side, axis, at, there in faces:
        @pl.when(jnp.logical_not(there))
        def _():
            for r in range(SWEEPS):
                halos[k][r, side] = jnp.zeros(halos[k].shape[2:], f32)
    size_x, size_y, size_z = m.shape[2:]
    lanes = zh.shape[-1]
    weight = OMEGA * flag_ref[...].astype(f32)
    rows = lax.broadcasted_iota(jnp.int32, (size_x, size_y, size_z), 1)
    cols = lax.broadcasted_iota(jnp.int32, (size_x, size_y, size_z), 2)
    swap.wait()
    now = [mine_ref[c] + back[c] for c in range(3)]
    for r in range(SWEEPS):
        for c in range(3):
            m[r, c] = now[c]
            yface[r, 0, c] = now[c][:, 0, :]
            yface[r, 1, c] = now[c][:, size_y - 1, :]
        copies = []
        for k, side, axis, at, there in faces:
            if k == 0:
                src = m.at[r, :, (size_x - 1) * side]
            elif k == 1:
                src = yface.at[r, side]
            else:
                src = m.at[r, :, :, :, pl.ds((size_z - lanes) * side, lanes)]
            out = pltpu.make_async_remote_copy(
                src_ref=src, dst_ref=halos[k].at[r, 1 - side], send_sem=zsend.at[r, k, side],
                recv_sem=sems.at[r + 1, k, 1 - side, 0], device_id={axis: at}, device_id_type=mesh_id)
            back_in = pltpu.make_async_remote_copy(
                src_ref=src, dst_ref=halos[k].at[r, side], send_sem=zsend.at[r, k, side],
                recv_sem=sems.at[r + 1, k, side, 0], device_id={axis: at}, device_id_type=mesh_id)
            pl.when(there)(out.start)
            copies.append((out, back_in, there))
        for out, back_in, there in copies:
            pl.when(there)(back_in.wait_recv)
            pl.when(there)(out.wait_send)
        later = []
        for c in range(3):
            v = now[c]
            total = jnp.concatenate([xh[r, 0, c][None], v[:-1]], 0)
            total = total + jnp.concatenate([v[1:], xh[r, 1, c][None]], 0)
            low = jnp.broadcast_to(yh[r, 0, c][:, None, :], v.shape)
            high = jnp.broadcast_to(yh[r, 1, c][:, None, :], v.shape)
            total = total + jnp.where(rows == 0, low, pltpu.roll(v, 1, 1))
            total = total + jnp.where(rows == size_y - 1, high, pltpu.roll(v, size_y - 1, 1))
            low = pltpu.roll(zh[r, 0, c], 1, 2)
            high = pltpu.roll(zh[r, 1, c], lanes - 1, 2)
            low = jnp.concatenate([low] * (size_z // lanes), 2)
            high = jnp.concatenate([high] * (size_z // lanes), 2)
            total = total + jnp.where(cols == 0, low, pltpu.roll(v, 1, 2))
            total = total + jnp.where(cols == size_z - 1, high, pltpu.roll(v, size_z - 1, 2))
            later.append(v + weight * (total * (1.0 / 6.0) - v))
        now = later
    for c in range(3):
        o_ref[c] = now[c]


SM = pl.BlockSpec(memory_space=pltpu.SMEM)
VM = pl.BlockSpec(memory_space=pltpu.VMEM)


ANY = pl.BlockSpec(memory_space=pl.ANY)


def gather_call(axes, half, nodes, pos, coef, pairs, live):
    ntiles = nodes.shape[1] * nodes.shape[2] // TILE
    spans = [len(shifts) for _, shifts, _ in axes]
    widest = max(spans)
    return pl.pallas_call(
        functools.partial(gather_kernel, axes, half),
        out_shape=(
            jax.ShapeDtypeStruct((ntiles, 16, TILE), f32),
            jax.ShapeDtypeStruct((spans[2], spans[1], spans[0], CT, 8, TILE), f32),
            jax.ShapeDtypeStruct((2,) + nodes.shape, f32),
            jax.ShapeDtypeStruct((8, pairs.shape[1]), jnp.int32),
        ),
        in_specs=[SM, SM, VM, VM, VM, VM],
        out_specs=(VM, ANY, ANY, ANY),
        scratch_shapes=[
            pltpu.VMEM((CT, 8, TILE), f32),
            pltpu.VMEM((8, pairs.shape[1]), jnp.int32),
            pltpu.SemaphoreType.DMA((3, widest)),
            pltpu.SemaphoreType.DMA((3, widest)),
            pltpu.SemaphoreType.DMA((2, 2)),
            pltpu.SemaphoreType.DMA((2,)),
        ],
        compiler_params=pltpu.CompilerParams(collective_id=0, has_side_effects=True),
        name="gather",
    )(pairs, live, nodes, pos, coef, pairs)


def rest_call(axes, half, pairs, live, mate_meta, x_both, table, init):
    shape = jax.ShapeDtypeStruct(x_both.shape[1:], f32)
    return pl.pallas_call(
        functools.partial(rest_kernel, axes, half),
        out_shape=(shape, shape),
        in_specs=[SM, SM, SM, VM, VM, VM],
        out_specs=(VM, VM),
        scratch_shapes=[pltpu.VMEM((2 * init.shape[0] + 1, 16, TILE), f32)],
        name="rest",
    )(pairs, live, mate_meta, x_both, table, init)


def smooth_call(half, sent, mine, flags):
    shape = mine.shape
    _, size_x, size_y, size_z = shape
    lanes = min(128, size_z)
    return pl.pallas_call(
        functools.partial(smooth_kernel, half),
        out_shape=jax.ShapeDtypeStruct(shape, f32),
        in_specs=[VM, VM, VM],
        out_specs=VM,
        scratch_shapes=[
            pltpu.VMEM(shape, f32),
            pltpu.VMEM((SWEEPS,) + shape, f32),
            pltpu.VMEM((SWEEPS, 2, 3, size_x, size_z), f32),
            pltpu.VMEM((SWEEPS, 2, 3, size_y, size_z), f32),
            pltpu.VMEM((SWEEPS, 2, 3, size_x, size_z), f32),
            pltpu.VMEM((SWEEPS, 2, 3, size_x, size_y, lanes), f32),
            pltpu.SemaphoreType.DMA((SWEEPS + 1, 3, 2, 1)),
            pltpu.SemaphoreType.DMA((SWEEPS, 3, 2)),
        ],
        compiler_params=pltpu.CompilerParams(collective_id=1, has_side_effects=True),
        name="smooth",
    )(sent, mine, flags)


def offsets(count, wanted):
    seen = []
    for d in wanted:
        if d % count not in seen:
            seen.append(d % count)
    return seen


def on_device(
    node_positions,
    control_positions,
    control_coefficient_values,
    support_pairs,
    live_counts,
    sliver_flags,
):
    size_x, size_y, size_z = node_positions.shape[1:]
    nx, ny, nz = (lax.axis_size(a) for a in ("gx", "gy", "gz"))
    half = nx // 2
    nodes = node_positions.reshape(3, size_x * size_y, size_z)
    axes = (
        ("gx", offsets(nx, (0, 1, -1, half, half + 1, half - 1)), True),
        ("gy", offsets(ny, (0, 1, -1)), ny <= 2),
        ("gz", offsets(nz, (0, 1, -1)), nz <= 2),
    )
    pairs = support_pairs.T
    first, table, x_both, mate_meta = gather_call(
        axes, half, nodes, control_positions, control_coefficient_values, pairs, live_counts
    )
    table = table.reshape((-1,) + table.shape[4:])
    sent, mine = rest_call(axes, half, pairs, live_counts, mate_meta, x_both, table, first)
    shape = node_positions.shape
    return smooth_call(half, sent.reshape(shape), mine.reshape(shape), sliver_flags)


def solution(mesh):
    return jax.shard_map(
        on_device,
        mesh=mesh,
        in_specs=(
            P(None, "gx", "gy", "gz"),
            P(None, ("gx", "gy", "gz")),
            P(None, ("gx", "gy", "gz")),
            P(("gx", "gy", "gz"), None),
            P(("gx", "gy", "gz")),
            P("gx", "gy", "gz"),
        ),
        out_specs=P(None, "gx", "gy", "gz"),
        check_vma=False,
    )
```

profile of v0, /device:TPU:0, one launch (start us, length us, event | category | flops | bytes accessed | tf_op | source)
XLA Modules:
  0.0 74.2 jit_solution(6881474872051612981)
XLA Ops:
  0.7 23.8 %gather.1 = (f32[32,16,512]{2,1,0:T(8,128)}, f32[2,3,4,4,8,512]{5,4,3,2,1,0:T(8,128)}, f32[2,3,64,256]{3,2,1,0:T(8,128)}, s32[8,128]{1,0:T(8,128)}) custom-call(s32[3,128]{1,0:T(4,128)} %bitcast.9, s32[1]{0:T(128)S(6)} %copy.8.live_ref.live, f32[3,64,256]{2,1,0:T(8,128)} %bitcast.6, f32[3,2048]{1,0:T(4,128)} %pos_ref.1, f32[3,2048]{1,0:T(4,128)} %coef_ref.1, ...), custom_call_target="tpu_custom_call" | custom-call | tf_op jit(solution)/shard_map/gather/pallas_call | solution.py:336
  24.4 28.2 %rest.1 = (f32[3,64,256]{2,1,0:T(8,128)}, f32[3,64,256]{2,1,0:T(8,128)}) custom-call(s32[3,128]{1,0:T(4,128)} %bitcast.11, s32[1]{0:T(128)S(6)} %copy.8.live_ref.live, s32[8,128]{1,0:T(8,128)} %get-tuple-element.11.mate_meta, f32[2,3,64,256]{3,2,1,0:T(8,128)} %get-tuple-element.12.x_both, f32[96,8,512]{2,1,0:T(8,128)} %bitcast.5, ...), custom_call_target="tpu_custom_call" | custom-call | tf_op jit(solution)/shard_map/rest/pallas_call | solution.py:361
  52.6 19.9 %smooth.1 = f32[3,8,8,256]{3,2,1,0:T(8,128)} custom-call(f32[3,8,8,256]{3,2,1,0:T(8,128)} %bitcast.7, f32[3,8,8,256]{3,2,1,0:T(8,128)} %bitcast.8, s32[8,8,256]{2,1,0:T(8,128)} %flag_ref.1), custom_call_target="tpu_custom_call" | custom-call | tf_op jit(solution)/shard_map/smooth/pallas_call | solution.py:375
  72.6 1.6 %copy.9 = f32[3,8,8,256]{3,2,1,0:T(8,128)} copy(f32[3,8,8,256]{3,2,1,0:T(8,128)} %smooth.1) | data formatting | bytes 393216
where the time goes:
time: 74.2 us
  Pallas kernels  71.9 us (97%)
  local copies, waits for them, and re-layouts  1.62 us (2%)
    pallas_call x1, Pallas kernels, rest_call(): pl.pallas_call(functools.partial(rest_kernel, axes, half), out_shape=(sha...  28.2 us
    pallas_call x1, Pallas kernels, gather_call(): pl.pallas_call(functools.partial(gather_kernel, axes, half), out_shape=(j...  23.8 us
    pallas_call x1, Pallas kernels, smooth_call(): pl.pallas_call(functools.partial(smooth_kernel, half), out_shape=jax.Shap...  19.9 us
    unnamed x1, local copies, waits for them, and re-layouts  1.62 us

commit v1 on v0

--- a/solution.py
+++ b/solution.py
@@ -13,8 +13,9 @@
 SWEEPS = 2
 RADIUS = 1.5
 OMEGA = 0.7
-GROUP = 4
+GROUP = 8
 HALF = 256
+FLOOR = 2.0**-21
 bf16, f32 = jnp.bfloat16, jnp.float32
 
 
@@ -50,24 +51,25 @@
     rows = row_ids()
     shift = jnp.where(rows == 0, origin[0], jnp.where(rows == 1, origin[1], origin[2]))
     pos = jnp.where(rows < 3, (raw - shift) * (1.0 / RADIUS), 0.0)
-    norm = jnp.sum(pos * pos, axis=0, keepdims=True)
+    norm = jnp.sum(pos * pos, axis=0, keepdims=True) + FLOOR
     block = jnp.where(rows == 3, 1.0, -2.0 * pos)
     block = jnp.where(rows == 4, jnp.broadcast_to(norm, (8, TILE)), block)
     a, b, c = split3(block)
     return jnp.transpose(jnp.concatenate([a, b, a, b, c, a], 0)).astype(bf16)
 
 
-def pair_sum(nodes, raw, origin):
-    controls = control_features(raw, origin)
+def coef_parts(raw):
     high = raw.astype(bf16).astype(f32)
-    coefs = jnp.concatenate([high, raw - high], 0).astype(bf16)
+    return jnp.concatenate([high, raw - high], 0).astype(bf16)
+
+
+def pair_sum(nodes, controls, coefs):
     coefs = jnp.concatenate([coefs, coefs], 1)
     sums = []
     for n in range(0, TILE, HALF):
         dist_sq = jnp.dot(controls, nodes[:, n : n + HALF], preferred_element_type=f32)
-        dist_sq = jnp.minimum(jnp.maximum(dist_sq, 1e-20), 1.0)
         scaled = dist_sq * lax.rsqrt(dist_sq)
-        fall = 1.0 - scaled
+        fall = jnp.maximum(1.0 - scaled, 0.0)
         fall2 = fall * fall
         weight = (fall2 * fall2) * (0.25 + scaled)
         top = weight.astype(bf16)
@@ -96,7 +98,7 @@
         pl.when(cond)(do)
 
 
-def gather_kernel(axes, half, slot_ref, live_ref, x_ref, pos_ref, coef_ref, pairs_ref, o_ref, table, x_both, mate_meta, own_ref, meta_ref, send, recv, extra, local):
+def gather_kernel(axes, half, slot_ref, live_ref, x_ref, pos_ref, coef_ref, pairs_ref, o_ref, table, x_both, mate_meta, own_ref, meta_ref, send, recv, extra, local, features, parts):
     origin = [lax.axis_index(axis).astype(f32) + 0.5 for axis, _, _ in axes]
     for s in range(CT):
         own_ref[s, 0:3] = pos_ref[:, s * TILE : (s + 1) * TILE]
@@ -158,25 +160,30 @@
 
     groups = o_ref.shape[0] // GROUP
 
-    def compute(low, high):
-        @pl.loop(low, high)
-        def _(g):
-            for j in range(GROUP):
-                i = g * GROUP + j
-                nodes = node_features(x_ref, i, origin)
-                o_ref[i] = pair_sum(nodes, own_ref[slot_ref[2, i]], origin)
-
-    cuts = [0, groups // 4, groups // 4 * 3, groups]
-    for k in range(3):
-        compute(cuts[k], cuts[k + 1])
-        if k == 0:
-            for copy in keep:
-                copy.wait()
-        land(k)
-        if k < 2:
-            start(k + 1)
-        if k == 0:
-            swaps[1].start()
+    for s in range(CT):
+        features[s] = control_features(own_ref[s], origin)
+        parts[s] = coef_parts(own_ref[s])
+
+    cuts = [groups // 4, groups // 4 * 3, groups]
+
+    @pl.loop(0, groups)
+    def _(g):
+        for j in range(GROUP):
+            i = g * GROUP + j
+            s = slot_ref[2, i]
+            o_ref[i] = pair_sum(node_features(x_ref, i, origin), features[s], parts[s])
+        for k in range(3):
+            @pl.when(g == cuts[k] - 1)
+            def _():
+                if k == 0:
+                    for copy in keep:
+                        copy.wait()
+                land(k)
+                if k < 2:
+                    start(k + 1)
+                if k == 0:
+                    swaps[1].start()
+
     for copy in swaps:
         copy.wait()
 
@@ -234,7 +241,8 @@
             ]
             nodes = node_features(x_both.at[part], t, origin)
             into = jnp.where(p < total, part * ntiles + t, trash)
-            acc[into] += pair_sum(nodes, table[source(owner, tile)], origin)
+            raw = table[source(owner, tile)]
+            acc[into] += pair_sum(nodes, control_features(raw, origin), coef_parts(raw))
 
     finish(acc, 0, sent_ref)
     finish(acc, ntiles, o_ref)
@@ -350,6 +358,8 @@
             pltpu.SemaphoreType.DMA((3, widest)),
             pltpu.SemaphoreType.DMA((2, 2)),
             pltpu.SemaphoreType.DMA((2,)),
+            pltpu.VMEM((CT, TILE, 48), bf16),
+            pltpu.VMEM((CT, 16, TILE), bf16),
         ],
         compiler_params=pltpu.CompilerParams(collective_id=0, has_side_effects=True),
         name="gather",

time: 74.2 us -> 68.9 us (0.929)
  Pallas kernels: 71.9 us -> 66.4 us
    pallas_call x1, Pallas kernels: 19.9 us -> 15.7 us  [smooth_call(): pl.pallas_call(functools.partial(smooth_kernel, half), out_shape=jax.Shap...]
    pallas_call x1, Pallas kernels: 23.8 us -> 21.8 us  [gather_call(): pl.pallas_call(functools.partial(gather_kernel, axes, half), out_shape=(j...]
where the time goes in v1:
time: 68.9 us; the launch traced here: 68.6 us
  Pallas kernels  66.4 us (96%)
  local copies, waits for them, and re-layouts  1.62 us (2%)
    pallas_call x1, Pallas kernels, rest_call(): pl.pallas_call(functools.partial(rest_kernel, axes, half), out_shape=(sha...  28.8 us
    pallas_call x1, Pallas kernels, gather_call(): pl.pallas_call(functools.partial(gather_kernel, axes, half), out_shape=(j...  21.8 us
    pallas_call x1, Pallas kernels, smooth_call(): pl.pallas_call(functools.partial(smooth_kernel, half), out_shape=jax.Shap...  15.7 us
    unnamed x1, local copies, waits for them, and re-layouts  1.62 us

profile of v1, /device:TPU:0, one launch (start us, length us, event | category | flops | bytes accessed | tf_op | source)
XLA Modules:
  0.0 68.6 jit_solution(2366674592715417333)
XLA Ops:
  0.7 21.8 %gather.1 = (f32[32,16,512]{2,1,0:T(8,128)}, f32[2,3,4,4,8,512]{5,4,3,2,1,0:T(8,128)}, f32[2,3,64,256]{3,2,1,0:T(8,128)}, s32[8,128]{1,0:T(8,128)}) custom-call(s32[3,128]{1,0:T(4,128)} %bitcast.9, s32[1]{0:T(128)S(6)} %copy.8.live_ref.live, f32[3,64,256]{2,1,0:T(8,128)} %bitcast.6, f32[3,2048]{1,0:T(4,128)} %pos_ref.1, f32[3,2048]{1,0:T(4,128)} %coef_ref.1, ...), custom_call_target="tpu_custom_call" | custom-call | tf_op jit(solution)/shard_map/gather/pallas_call | solution.py:344
  22.5 28.8 %rest.1 = (f32[3,64,256]{2,1,0:T(8,128)}, f32[3,64,256]{2,1,0:T(8,128)}) custom-call(s32[3,128]{1,0:T(4,128)} %bitcast.11, s32[1]{0:T(128)S(6)} %copy.8.live_ref.live, s32[8,128]{1,0:T(8,128)} %get-tuple-element.11.mate_meta, f32[2,3,64,256]{3,2,1,0:T(8,128)} %get-tuple-element.12.x_both, f32[96,8,512]{2,1,0:T(8,128)} %bitcast.5, ...), custom_call_target="tpu_custom_call" | custom-call | tf_op jit(solution)/shard_map/rest/pallas_call | solution.py:371
  51.3 15.7 %smooth.1 = f32[3,8,8,256]{3,2,1,0:T(8,128)} custom-call(f32[3,8,8,256]{3,2,1,0:T(8,128)} %bitcast.7, f32[3,8,8,256]{3,2,1,0:T(8,128)} %bitcast.8, s32[8,8,256]{2,1,0:T(8,128)} %flag_ref.1), custom_call_target="tpu_custom_call" | custom-call | tf_op jit(solution)/shard_map/smooth/pallas_call | solution.py:385
  67.0 1.6 %copy.9 = f32[3,8,8,256]{3,2,1,0:T(8,128)} copy(f32[3,8,8,256]{3,2,1,0:T(8,128)} %smooth.1) | data formatting | bytes 393216

commit v2 on v1

--- a/solution.py
+++ b/solution.py
@@ -14,6 +14,8 @@
 RADIUS = 1.5
 OMEGA = 0.7
 GROUP = 8
+STEP = 4
+LATE = 8
 HALF = 256
 FLOOR = 2.0**-21
 bf16, f32 = jnp.bfloat16, jnp.float32
@@ -80,6 +82,20 @@
     return jnp.concatenate(sums, 1)
 
 
+def own_tiles(own_ref, pos_ref, coef_ref, features, parts, origin):
+    for s in range(CT):
+        own_ref[s, 0:3] = pos_ref[:, s * TILE : (s + 1) * TILE]
+        own_ref[s, 3:6] = coef_ref[:, s * TILE : (s + 1) * TILE]
+        own_ref[s, 6:8] = jnp.zeros((2, TILE), f32)
+    for s in range(CT):
+        features[s] = control_features(own_ref[s], origin)
+        parts[s] = coef_parts(own_ref[s])
+
+
+def merged(both):
+    return 4.0 * (both[:8] + both[8:])
+
+
 def peers(axis, shifts, wrap):
     count, me = lax.axis_size(axis), lax.axis_index(axis)
     for i, d in enumerate(shifts):
@@ -91,6 +107,12 @@
         yield i, (me + step + count) % count, (me - step + count) % count, ahead, behind
 
 
+def both_of(a, b):
+    if a is None or b is None:
+        return b if a is None else a
+    return jnp.logical_and(a, b)
+
+
 def when(cond, do):
     if cond is None:
         do()
@@ -100,10 +122,7 @@
 
 def gather_kernel(axes, half, slot_ref, live_ref, x_ref, pos_ref, coef_ref, pairs_ref, o_ref, table, x_both, mate_meta, own_ref, meta_ref, send, recv, extra, local, features, parts):
     origin = [lax.axis_index(axis).astype(f32) + 0.5 for axis, _, _ in axes]
-    for s in range(CT):
-        own_ref[s, 0:3] = pos_ref[:, s * TILE : (s + 1) * TILE]
-        own_ref[s, 3:6] = coef_ref[:, s * TILE : (s + 1) * TILE]
-        own_ref[s, 6:8] = jnp.zeros((2, TILE), f32)
+    own_tiles(own_ref, pos_ref, coef_ref, features, parts, origin)
     meta_ref[0:3] = pairs_ref[...]
     meta_ref[3:8] = jnp.full((5, meta_ref.shape[1]), live_ref[0], jnp.int32)
     barrier = pltpu.get_barrier_semaphore()
@@ -115,30 +134,37 @@
             expected = expected + (1 if there is None else there.astype(jnp.int32))
     pl.semaphore_wait(barrier, expected)
 
-    def views(k, i):
-        if k == 0:
-            return own_ref, table.at[0, 0, i]
-        if k == 1:
-            return table.at[0, 0], table.at[0, i]
-        return table.at[0], table.at[i]
-
-    def copies(k):
+    wide = [len(shifts) for _, shifts, _ in axes]
+    columns = [(i1, i0) for i1 in range(wide[1]) for i0 in range(wide[0])]
+    came = {0: None}
+    for i, _, _, has_ahead, _ in peers(*axes[1]):
+        came[i] = has_ahead
+
+    def copies(k, blocks):
         axis, shifts, wrap = axes[k]
         for i, ahead, behind, has_ahead, has_behind in peers(axis, shifts, wrap):
-            src, dst = views(k, i)
-            copy = pltpu.make_async_remote_copy(
-                src_ref=src, dst_ref=dst, send_sem=send.at[k, i], recv_sem=recv.at[k, i],
-                device_id={axis: behind}, device_id_type=pl.DeviceIdType.MESH)
-            yield copy, has_behind, has_ahead
-
-    def start(k):
-        for copy, goes, _ in copies(k):
+            for i1, i0 in blocks:
+                src = table.at[0, i1, i0] if i1 or i0 else own_ref
+                dst = table.at[(0, 0, i) if k == 0 else (0, i, i0) if k == 1 else (i, i1, i0)]
+                n = i1 * wide[0] + i0
+                copy = pltpu.make_async_remote_copy(
+                    src_ref=src, dst_ref=dst, send_sem=send.at[k, i, n], recv_sem=recv.at[k, i, n],
+                    device_id={axis: behind}, device_id_type=pl.DeviceIdType.MESH)
+                yield copy, both_of(has_behind, came[i1]), both_of(has_ahead, came[i1])
+
+    def start(k, blocks):
+        for copy, goes, _ in copies(k, blocks):
             when(goes, copy.start)
 
-    def land(k):
-        for copy, goes, comes in copies(k):
+    def land(k, blocks):
+        for copy, goes, comes in copies(k, blocks):
             when(comes, copy.wait_recv)
             when(goes, copy.wait_send)
+
+    near = [(0, 0)]
+    row = [(0, i0) for i0 in range(1, wide[0])]
+    side = [(i1, 0) for i1 in range(1, wide[1])]
+    far = [(i1, i0) for i1, i0 in columns if i1 and i0]
 
     gx_name = axes[0][0]
     count = lax.axis_size(gx_name)
@@ -147,9 +173,10 @@
         pltpu.make_async_copy(own_ref, table.at[0, 0, 0], local.at[0]),
         pltpu.make_async_copy(x_ref, x_both.at[1], local.at[1]),
     ]
+    for k in range(3):
+        start(k, near)
     for copy in keep:
         copy.start()
-    start(0)
     swaps = [
         pltpu.make_async_remote_copy(
             src_ref=src, dst_ref=dst, send_sem=extra.at[0, n], recv_sem=extra.at[1, n],
@@ -158,32 +185,31 @@
     ]
     swaps[0].start()
 
-    groups = o_ref.shape[0] // GROUP
-
-    for s in range(CT):
-        features[s] = control_features(own_ref[s], origin)
-        parts[s] = coef_parts(own_ref[s])
-
-    cuts = [groups // 4, groups // 4 * 3, groups]
+    groups = o_ref.shape[0] // STEP
 
     @pl.loop(0, groups)
     def _(g):
-        for j in range(GROUP):
-            i = g * GROUP + j
+        for j in range(STEP):
+            i = g * STEP + j
             s = slot_ref[2, i]
-            o_ref[i] = pair_sum(node_features(x_ref, i, origin), features[s], parts[s])
-        for k in range(3):
-            @pl.when(g == cuts[k] - 1)
-            def _():
-                if k == 0:
-                    for copy in keep:
-                        copy.wait()
-                land(k)
-                if k < 2:
-                    start(k + 1)
-                if k == 0:
-                    swaps[1].start()
-
+            o_ref[i] = merged(pair_sum(node_features(x_ref, i, origin), features[s], parts[s]))
+
+        @pl.when(g == groups // 3 - 1)
+        def _():
+            for copy in keep:
+                copy.wait()
+            land(0, near)
+            start(1, row)
+            land(1, near)
+            start(2, row + side)
+            swaps[1].start()
+
+        @pl.when(g == groups - 2)
+        def _():
+            land(1, row)
+            start(2, far)
+
+    land(2, columns)
     for copy in swaps:
         copy.wait()
 
@@ -192,16 +218,15 @@
     per = TILE // o_ref.shape[2]
     width = o_ref.shape[2]
     for t in range(o_ref.shape[1] // per):
-        both = 4.0 * (acc[at + t, :8] + acc[at + t, 8:])
+        both = merged(acc[at + t])
         for j in range(per):
             o_ref[:, t * per + j, :] = both[3:6, j * width : (j + 1) * width]
 
 
-def rest_kernel(axes, half, meta, live, mate_meta, x_both, table, init, sent_ref, o_ref, acc):
-    ntiles = init.shape[0]
-    trash = 2 * ntiles
-    acc[:ntiles] = jnp.zeros_like(init)
-    acc[ntiles:trash] = init[...]
+def rest_kernel(axes, half, meta, live, mate_meta, x_both, table, sent_ref, o_ref, acc):
+    trash = acc.shape[0] - 1
+    ntiles = trash // 2
+    acc[:trash] = jnp.zeros((trash,) + acc.shape[1:], f32)
     here = [lax.axis_index(axis) for axis, _, _ in axes]
     counts = [lax.axis_size(axis) for axis, _, _ in axes]
     mate_at = lax.rem(here[0] + half, counts[0])
@@ -248,7 +273,7 @@
     finish(acc, ntiles, o_ref)
 
 
-def smooth_kernel(half, sent_ref, mine_ref, flag_ref, o_ref, back, m, yface, xh, yh, zh, sems, zsend):
+def smooth_kernel(half, slot_ref, x_ref, pos_ref, coef_ref, first_ref, sent_ref, mine_ref, flag_ref, o_ref, back, m, yface, xh, yh, zh, sems, zsend, own_ref, features, parts, rbf):
     names = ("gx", "gy", "gz")
     here = [lax.axis_index(a) for a in names]
     counts = [lax.axis_size(a) for a in names]
@@ -281,10 +306,23 @@
     size_x, size_y, size_z = m.shape[2:]
     lanes = zh.shape[-1]
     weight = OMEGA * flag_ref[...].astype(f32)
+    origin = [at.astype(f32) + 0.5 for at in here]
+    own_tiles(own_ref, pos_ref, coef_ref, features, parts, origin)
+    per = TILE // size_z
+    early = first_ref.shape[0]
+    for t in range(early + LATE):
+        if t < early:
+            both = first_ref[t]
+        else:
+            s = slot_ref[2, t]
+            both = merged(pair_sum(node_features(x_ref, t, origin), features[s], parts[s]))
+        for j in range(per):
+            at = t * per + j
+            rbf[:, at // size_y, at % size_y, :] = both[3:6, j * size_z : (j + 1) * size_z]
     rows = lax.broadcasted_iota(jnp.int32, (size_x, size_y, size_z), 1)
     cols = lax.broadcasted_iota(jnp.int32, (size_x, size_y, size_z), 2)
     swap.wait()
-    now = [mine_ref[c] + back[c] for c in range(3)]
+    now = [rbf[c] + (mine_ref[c] + back[c]) for c in range(3)]
     for r in range(SWEEPS):
         for c in range(3):
             m[r, c] = now[c]
@@ -344,7 +382,7 @@
     return pl.pallas_call(
         functools.partial(gather_kernel, axes, half),
         out_shape=(
-            jax.ShapeDtypeStruct((ntiles, 16, TILE), f32),
+            jax.ShapeDtypeStruct((ntiles - LATE, 8, TILE), f32),
             jax.ShapeDtypeStruct((spans[2], spans[1], spans[0], CT, 8, TILE), f32),
             jax.ShapeDtypeStruct((2,) + nodes.shape, f32),
             jax.ShapeDtypeStruct((8, pairs.shape[1]), jnp.int32),
@@ -354,8 +392,8 @@
         scratch_shapes=[
             pltpu.VMEM((CT, 8, TILE), f32),
             pltpu.VMEM((8, pairs.shape[1]), jnp.int32),
-            pltpu.SemaphoreType.DMA((3, widest)),
-            pltpu.SemaphoreType.DMA((3, widest)),
+            pltpu.SemaphoreType.DMA((3, widest, spans[0] * spans[1])),
+            pltpu.SemaphoreType.DMA((3, widest, spans[0] * spans[1])),
             pltpu.SemaphoreType.DMA((2, 2)),
             pltpu.SemaphoreType.DMA((2,)),
             pltpu.VMEM((CT, TILE, 48), bf16),
@@ -366,26 +404,27 @@
     )(pairs, live, nodes, pos, coef, pairs)
 
 
-def rest_call(axes, half, pairs, live, mate_meta, x_both, table, init):
+def rest_call(axes, half, pairs, live, mate_meta, x_both, table):
+    ntiles = x_both.shape[2] * x_both.shape[3] // TILE
     shape = jax.ShapeDtypeStruct(x_both.shape[1:], f32)
     return pl.pallas_call(
         functools.partial(rest_kernel, axes, half),
         out_shape=(shape, shape),
-        in_specs=[SM, SM, SM, VM, VM, VM],
+        in_specs=[SM, SM, SM, VM, VM],
         out_specs=(VM, VM),
-        scratch_shapes=[pltpu.VMEM((2 * init.shape[0] + 1, 16, TILE), f32)],
+        scratch_shapes=[pltpu.VMEM((2 * ntiles + 1, 16, TILE), f32)],
         name="rest",
-    )(pairs, live, mate_meta, x_both, table, init)
-
-
-def smooth_call(half, sent, mine, flags):
+    )(pairs, live, mate_meta, x_both, table)
+
+
+def smooth_call(half, pairs, nodes, pos, coef, first, sent, mine, flags):
     shape = mine.shape
     _, size_x, size_y, size_z = shape
     lanes = min(128, size_z)
     return pl.pallas_call(
         functools.partial(smooth_kernel, half),
         out_shape=jax.ShapeDtypeStruct(shape, f32),
-        in_specs=[VM, VM, VM],
+        in_specs=[SM] + [VM] * 7,
         out_specs=VM,
         scratch_shapes=[
             pltpu.VMEM(shape, f32),
@@ -396,10 +435,14 @@
             pltpu.VMEM((SWEEPS, 2, 3, size_x, size_y, lanes), f32),
             pltpu.SemaphoreType.DMA((SWEEPS + 1, 3, 2, 1)),
             pltpu.SemaphoreType.DMA((SWEEPS, 3, 2)),
+            pltpu.VMEM((CT, 8, TILE), f32),
+            pltpu.VMEM((CT, TILE, 48), bf16),
+            pltpu.VMEM((CT, 16, TILE), bf16),
+            pltpu.VMEM(shape, f32),
         ],
         compiler_params=pltpu.CompilerParams(collective_id=1, has_side_effects=True),
         name="smooth",
-    )(sent, mine, flags)
+    )(pairs, nodes, pos, coef, first, sent, mine, flags)
 
 
 def offsets(count, wanted):
@@ -432,9 +475,12 @@
         axes, half, nodes, control_positions, control_coefficient_values, pairs, live_counts
     )
     table = table.reshape((-1,) + table.shape[4:])
-    sent, mine = rest_call(axes, half, pairs, live_counts, mate_meta, x_both, table, first)
+    sent, mine = rest_call(axes, half, pairs, live_counts, mate_meta, x_both, table)
     shape = node_positions.shape
-    return smooth_call(half, sent.reshape(shape), mine.reshape(shape), sliver_flags)
+    return smooth_call(
+        half, pairs, nodes, control_positions, control_coefficient_values, first,
+        sent.reshape(shape), mine.reshape(shape), sliver_flags,
+    )
 
 
 def solution(mesh):

time: 68.9 us -> 68.7 us (level)
    pallas_call x1, Pallas kernels: 15.7 us -> 16.5 us  [smooth_call(): pl.pallas_call(functools.partial(smooth_kernel, half), out_shape=jax.Shap...]
where the time goes in v2:
time: 68.7 us; the launch traced here: 68.5 us
  Pallas kernels  66.2 us (96%)
  local copies, waits for them, and re-layouts  1.62 us (2%)
    pallas_call x1, Pallas kernels, rest_call(): pl.pallas_call(functools.partial(rest_kernel, axes, half), out_shape=(sha...  28.6 us
    pallas_call x1, Pallas kernels, gather_call(): pl.pallas_call(functools.partial(gather_kernel, axes, half), out_shape=(j...  21.2 us
    pallas_call x1, Pallas kernels, smooth_call(): pl.pallas_call(functools.partial(smooth_kernel, half), out_shape=jax.Shap...  16.5 us
    unnamed x1, local copies, waits for them, and re-layouts  1.62 us

profile of v2, /device:TPU:0, one launch (start us, length us, event | category | flops | bytes accessed | tf_op | source)
XLA Modules:
  0.0 68.5 jit_solution(6468041878704429470)
XLA Ops:
  0.7 21.2 %gather.1 = (f32[24,8,512]{2,1,0:T(8,128)}, f32[2,3,4,4,8,512]{5,4,3,2,1,0:T(8,128)}, f32[2,3,64,256]{3,2,1,0:T(8,128)}, s32[8,128]{1,0:T(8,128)}) custom-call(s32[3,128]{1,0:T(4,128)} %bitcast.10, s32[1]{0:T(128)S(6)} %copy.8.live_ref.live, f32[3,64,256]{2,1,0:T(8,128)} %bitcast.6, f32[3,2048]{1,0:T(4,128)} %pos_ref.3, f32[3,2048]{1,0:T(4,128)} %coef_ref.3, ...), custom_call_target="tpu_custom_call" | custom-call | tf_op jit(solution)/shard_map/gather/pallas_call | solution.py:382
  21.9 28.6 %rest.1 = (f32[3,64,256]{2,1,0:T(8,128)}, f32[3,64,256]{2,1,0:T(8,128)}) custom-call(s32[3,128]{1,0:T(4,128)} %bitcast.12, s32[1]{0:T(128)S(6)} %copy.8.live_ref.live, s32[8,128]{1,0:T(8,128)} %get-tuple-element.12.mate_meta, f32[2,3,64,256]{3,2,1,0:T(8,128)} %get-tuple-element.13.x_both, f32[96,8,512]{2,1,0:T(8,128)} %bitcast.5), custom_call_target="tpu_custom_call" | custom-call | tf_op jit(solution)/shard_map/rest/pallas_call | solution.py:410
  50.4 16.5 %smooth.1 = f32[3,8,8,256]{3,2,1,0:T(8,128)} custom-call(s32[3,128]{1,0:T(4,128)} %bitcast.13, f32[3,64,256]{2,1,0:T(8,128)} %bitcast.7, f32[3,2048]{1,0:T(4,128)} %pos_ref.3, f32[3,2048]{1,0:T(4,128)} %coef_ref.3, f32[24,8,512]{2,1,0:T(8,128)} %get-tuple-element.11.first_ref, f32[3,8,8,256]{3,2,1,0:T(8,128)} %bitcast.8, f32[3,8,8,256]{3,2,1,0:T(8,128)} %bitcast.9, ...), custom_call_target="tpu_custom_call" | custom-call | tf_op jit(solution)/shard_map/smooth/pallas_call | solution.py:424
  66.9 1.6 %copy.9 = f32[3,8,8,256]{3,2,1,0:T(8,128)} copy(f32[3,8,8,256]{3,2,1,0:T(8,128)} %smooth.1) | data formatting | bytes 393216

commit v3 on v2

--- a/solution.py
+++ b/solution.py
@@ -15,7 +15,7 @@
 OMEGA = 0.7
 GROUP = 8
 STEP = 4
-LATE = 8
+LATE = 12
 HALF = 256
 FLOOR = 2.0**-21
 bf16, f32 = jnp.bfloat16, jnp.float32
@@ -82,14 +82,30 @@
     return jnp.concatenate(sums, 1)
 
 
-def own_tiles(own_ref, pos_ref, coef_ref, features, parts, origin):
+def own_tiles(pos_ref, coef_ref, features, parts, origin):
     for s in range(CT):
-        own_ref[s, 0:3] = pos_ref[:, s * TILE : (s + 1) * TILE]
-        own_ref[s, 3:6] = coef_ref[:, s * TILE : (s + 1) * TILE]
-        own_ref[s, 6:8] = jnp.zeros((2, TILE), f32)
-    for s in range(CT):
-        features[s] = control_features(own_ref[s], origin)
-        parts[s] = coef_parts(own_ref[s])
+        at = slice(s * TILE, (s + 1) * TILE)
+        raw = jnp.concatenate([pos_ref[:, at], coef_ref[:, at], jnp.zeros((2, TILE), f32)], 0)
+        features[s] = control_features(raw, origin)
+        parts[s] = coef_parts(raw)
+
+
+def pack_tiles(pos_ref, coef_ref, own_ref):
+    last = slice((CT - 1) * TILE, CT * TILE)
+    for s in range(CT - 1):
+        at = slice(s * TILE, (s + 1) * TILE)
+        own_ref[s, 0:3] = pos_ref[:, at]
+        own_ref[s, 3:6] = coef_ref[:, at]
+        for j in range(2):
+            c = 2 * s + j
+            own_ref[s, 6 + j : 7 + j] = pos_ref[c : c + 1, last] if c < 3 else coef_ref[c - 3 : c - 2, last]
+
+
+def tile_rows(table, block, slot):
+    first = block * (CT - 1)
+    whole = table[first + jnp.minimum(slot, CT - 2)]
+    last = jnp.concatenate([table[first + s, 6:8] for s in range(CT - 1)] + [jnp.zeros((2, TILE), f32)], 0)
+    return jnp.where(slot == CT - 1, last, whole)
 
 
 def merged(both):
@@ -122,9 +138,6 @@
 
 def gather_kernel(axes, half, slot_ref, live_ref, x_ref, pos_ref, coef_ref, pairs_ref, o_ref, table, x_both, mate_meta, own_ref, meta_ref, send, recv, extra, local, features, parts):
     origin = [lax.axis_index(axis).astype(f32) + 0.5 for axis, _, _ in axes]
-    own_tiles(own_ref, pos_ref, coef_ref, features, parts, origin)
-    meta_ref[0:3] = pairs_ref[...]
-    meta_ref[3:8] = jnp.full((5, meta_ref.shape[1]), live_ref[0], jnp.int32)
     barrier = pltpu.get_barrier_semaphore()
     expected = 0
     for axis, shifts, wrap in axes:
@@ -132,6 +145,9 @@
             when(there, lambda axis=axis, ahead=ahead: pl.semaphore_signal(
                 barrier, inc=1, device_id={axis: ahead}, device_id_type=pl.DeviceIdType.MESH))
             expected = expected + (1 if there is None else there.astype(jnp.int32))
+    meta_ref[0:3] = pairs_ref[...]
+    meta_ref[3:8] = jnp.full((5, meta_ref.shape[1]), live_ref[0], jnp.int32)
+    pack_tiles(pos_ref, coef_ref, own_ref)
     pl.semaphore_wait(barrier, expected)
 
     wide = [len(shifts) for _, shifts, _ in axes]
@@ -140,10 +156,10 @@
     for i, _, _, has_ahead, _ in peers(*axes[1]):
         came[i] = has_ahead
 
-    def copies(k, blocks):
+    def copies(k, blocks, only=None):
         axis, shifts, wrap = axes[k]
         for i, ahead, behind, has_ahead, has_behind in peers(axis, shifts, wrap):
-            for i1, i0 in blocks:
+            for i1, i0 in blocks if only is None or i in only else ():
                 src = table.at[0, i1, i0] if i1 or i0 else own_ref
                 dst = table.at[(0, 0, i) if k == 0 else (0, i, i0) if k == 1 else (i, i1, i0)]
                 n = i1 * wide[0] + i0
@@ -156,15 +172,22 @@
         for copy, goes, _ in copies(k, blocks):
             when(goes, copy.start)
 
-    def land(k, blocks):
-        for copy, goes, comes in copies(k, blocks):
+    def land(k, blocks, only=None):
+        for copy, _, comes in copies(k, blocks, only):
             when(comes, copy.wait_recv)
+
+    def drain(k, blocks):
+        for copy, goes, _ in copies(k, blocks):
             when(goes, copy.wait_send)
+
+    def relay(i0):
+        land(0, near, (i0,))
+        start(1, [(0, i0)])
+        start(2, [(0, i0)])
 
     near = [(0, 0)]
     row = [(0, i0) for i0 in range(1, wide[0])]
     side = [(i1, 0) for i1 in range(1, wide[1])]
-    far = [(i1, i0) for i1, i0 in columns if i1 and i0]
 
     gx_name = axes[0][0]
     count = lax.axis_size(gx_name)
@@ -185,7 +208,10 @@
     ]
     swaps[0].start()
 
+    own_tiles(pos_ref, coef_ref, features, parts, origin)
     groups = o_ref.shape[0] // STEP
+    direct = [i for i, d in enumerate(axes[0][1]) if d == half]
+    others = [i for i in range(1, wide[0]) if i not in direct]
 
     @pl.loop(0, groups)
     def _(g):
@@ -194,22 +220,26 @@
             s = slot_ref[2, i]
             o_ref[i] = merged(pair_sum(node_features(x_ref, i, origin), features[s], parts[s]))
 
-        @pl.when(g == groups // 3 - 1)
+        @pl.when(g == 1)
         def _():
+            for i0 in direct + others:
+                relay(i0)
+            swaps[1].start()
             for copy in keep:
                 copy.wait()
-            land(0, near)
-            start(1, row)
             land(1, near)
-            start(2, row + side)
-            swaps[1].start()
-
-        @pl.when(g == groups - 2)
+            start(2, side)
+
+        @pl.when(g == 3)
         def _():
-            land(1, row)
-            start(2, far)
+            for i0 in direct + others:
+                land(1, [(0, i0)])
+                start(2, [(i1, i0) for i1 in range(1, wide[1])])
 
     land(2, columns)
+    drain(0, near)
+    drain(1, near + row)
+    drain(2, columns)
     for copy in swaps:
         copy.wait()
 
@@ -236,7 +266,7 @@
     helped = theirs - skip
     total = helped + jnp.minimum(mine, goal) - ntiles
 
-    def source(owner, slot):
+    def source(owner):
         owners = (
             lax.div(owner, counts[1] * counts[2]),
             lax.rem(lax.div(owner, counts[2]), counts[1]),
@@ -247,7 +277,7 @@
             shifts = axes[k][1]
             rel = lax.rem(owners[k] - here[k] + counts[k], counts[k])
             at = at * len(shifts) + sum(jnp.where(rel == d, i, 0) for i, d in enumerate(shifts))
-        return at * CT + slot
+        return at
 
     @pl.loop(0, lax.div(total + GROUP - 1, GROUP))
     def _(g):
@@ -266,14 +296,14 @@
             ]
             nodes = node_features(x_both.at[part], t, origin)
             into = jnp.where(p < total, part * ntiles + t, trash)
-            raw = table[source(owner, tile)]
+            raw = tile_rows(table, source(owner), tile)
             acc[into] += pair_sum(nodes, control_features(raw, origin), coef_parts(raw))
 
     finish(acc, 0, sent_ref)
     finish(acc, ntiles, o_ref)
 
 
-def smooth_kernel(half, slot_ref, x_ref, pos_ref, coef_ref, first_ref, sent_ref, mine_ref, flag_ref, o_ref, back, m, yface, xh, yh, zh, sems, zsend, own_ref, features, parts, rbf):
+def smooth_kernel(half, slot_ref, x_ref, pos_ref, coef_ref, first_ref, sent_ref, mine_ref, flag_ref, o_ref, back, m, yface, xh, yh, zh, sems, zsend, features, parts, rbf):
     names = ("gx", "gy", "gz")
     here = [lax.axis_index(a) for a in names]
     counts = [lax.axis_size(a) for a in names]
@@ -307,7 +337,7 @@
     lanes = zh.shape[-1]
     weight = OMEGA * flag_ref[...].astype(f32)
     origin = [at.astype(f32) + 0.5 for at in here]
-    own_tiles(own_ref, pos_ref, coef_ref, features, parts, origin)
+    own_tiles(pos_ref, coef_ref, features, parts, origin)
     per = TILE // size_z
     early = first_ref.shape[0]
     for t in range(early + LATE):
@@ -383,14 +413,14 @@
         functools.partial(gather_kernel, axes, half),
         out_shape=(
             jax.ShapeDtypeStruct((ntiles - LATE, 8, TILE), f32),
-            jax.ShapeDtypeStruct((spans[2], spans[1], spans[0], CT, 8, TILE), f32),
+            jax.ShapeDtypeStruct((spans[2], spans[1], spans[0], CT - 1, 8, TILE), f32),
             jax.ShapeDtypeStruct((2,) + nodes.shape, f32),
             jax.ShapeDtypeStruct((8, pairs.shape[1]), jnp.int32),
         ),
         in_specs=[SM, SM, VM, VM, VM, VM],
         out_specs=(VM, ANY, ANY, ANY),
         scratch_shapes=[
-            pltpu.VMEM((CT, 8, TILE), f32),
+            pltpu.VMEM((CT - 1, 8, TILE), f32),
             pltpu.VMEM((8, pairs.shape[1]), jnp.int32),
             pltpu.SemaphoreType.DMA((3, widest, spans[0] * spans[1])),
             pltpu.SemaphoreType.DMA((3, widest, spans[0] * spans[1])),
@@ -435,7 +465,6 @@
             pltpu.VMEM((SWEEPS, 2, 3, size_x, size_y, lanes), f32),
             pltpu.SemaphoreType.DMA((SWEEPS + 1, 3, 2, 1)),
             pltpu.SemaphoreType.DMA((SWEEPS, 3, 2)),
-            pltpu.VMEM((CT, 8, TILE), f32),
             pltpu.VMEM((CT, TILE, 48), bf16),
             pltpu.VMEM((CT, 16, TILE), bf16),
             pltpu.VMEM(shape, f32),

time: 68.7 us -> 66.9 us (0.974)
  Pallas kernels: 66.2 us -> 64.4 us
    pallas_call x1, Pallas kernels: 28.6 us -> 24.9 us  [rest_call(): pl.pallas_call(functools.partial(rest_kernel, axes, half), out_shape=(sha...]
    pallas_call x1, Pallas kernels: 16.5 us -> 19.8 us  [smooth_call(): pl.pallas_call(functools.partial(smooth_kernel, half), out_shape=jax.Shap...]
    pallas_call x1, Pallas kernels: 21.2 us -> 19.7 us  [gather_call(): pl.pallas_call(functools.partial(gather_kernel, axes, half), out_shape=(j...]
where the time goes in v3:
time: 66.9 us; the launch traced here: 66.7 us
  Pallas kernels  64.4 us (96%)
  local copies, waits for them, and re-layouts  1.62 us (2%)
  between operations  0.67 us (1%)
    pallas_call x1, Pallas kernels, rest_call(): pl.pallas_call(functools.partial(rest_kernel, axes, half), out_shape=(sha...  24.9 us
    pallas_call x1, Pallas kernels, smooth_call(): pl.pallas_call(functools.partial(smooth_kernel, half), out_shape=jax.Shap...  19.8 us
    pallas_call x1, Pallas kernels, gather_call(): pl.pallas_call(functools.partial(gather_kernel, axes, half), out_shape=(j...  19.7 us
    unnamed x1, local copies, waits for them, and re-layouts  1.62 us

profile of v3, /device:TPU:0, one launch (start us, length us, event | category | flops | bytes accessed | tf_op | source)
XLA Modules:
  0.0 66.7 jit_solution(12890040145294045106)
XLA Ops:
  0.7 19.7 %gather.1 = (f32[20,8,512]{2,1,0:T(8,128)}, f32[2,3,4,3,8,512]{5,4,3,2,1,0:T(8,128)}, f32[2,3,64,256]{3,2,1,0:T(8,128)}, s32[8,128]{1,0:T(8,128)}) custom-call(s32[3,128]{1,0:T(4,128)} %bitcast.10, s32[1]{0:T(128)S(6)} %copy.8.live_ref.live, f32[3,64,256]{2,1,0:T(8,128)} %bitcast.6, f32[3,2048]{1,0:T(4,128)} %pos_ref.3, f32[3,2048]{1,0:T(4,128)} %coef_ref.3, ...), custom_call_target="tpu_custom_call" | custom-call | tf_op jit(solution)/shard_map/gather/pallas_call | solution.py:412
  20.4 24.9 %rest.1 = (f32[3,64,256]{2,1,0:T(8,128)}, f32[3,64,256]{2,1,0:T(8,128)}) custom-call(s32[3,128]{1,0:T(4,128)} %bitcast.12, s32[1]{0:T(128)S(6)} %copy.8.live_ref.live, s32[8,128]{1,0:T(8,128)} %get-tuple-element.12.mate_meta, f32[2,3,64,256]{3,2,1,0:T(8,128)} %get-tuple-element.13.x_both, f32[72,8,512]{2,1,0:T(8,128)} %bitcast.5), custom_call_target="tpu_custom_call" | custom-call | tf_op jit(solution)/shard_map/rest/pallas_call | solution.py:440
  45.3 19.8 %smooth.1 = f32[3,8,8,256]{3,2,1,0:T(8,128)} custom-call(s32[3,128]{1,0:T(4,128)} %bitcast.13, f32[3,64,256]{2,1,0:T(8,128)} %bitcast.7, f32[3,2048]{1,0:T(4,128)} %pos_ref.3, f32[3,2048]{1,0:T(4,128)} %coef_ref.3, f32[20,8,512]{2,1,0:T(8,128)} %get-tuple-element.11.first_ref, f32[3,8,8,256]{3,2,1,0:T(8,128)} %bitcast.8, f32[3,8,8,256]{3,2,1,0:T(8,128)} %bitcast.9, ...), custom_call_target="tpu_custom_call" | custom-call | tf_op jit(solution)/shard_map/smooth/pallas_call | solution.py:454
  65.0 1.6 %copy.9 = f32[3,8,8,256]{3,2,1,0:T(8,128)} copy(f32[3,8,8,256]{3,2,1,0:T(8,128)} %smooth.1) | data formatting | bytes 393216

commit v4 on v3

--- a/solution.py
+++ b/solution.py
@@ -102,9 +102,8 @@
 
 
 def tile_rows(table, block, slot):
-    first = block * (CT - 1)
-    whole = table[first + jnp.minimum(slot, CT - 2)]
-    last = jnp.concatenate([table[first + s, 6:8] for s in range(CT - 1)] + [jnp.zeros((2, TILE), f32)], 0)
+    whole = table[block + (jnp.minimum(slot, CT - 2),)]
+    last = jnp.concatenate([table[block + (s, slice(6, 8))] for s in range(CT - 1)] + [jnp.zeros((2, TILE), f32)], 0)
     return jnp.where(slot == CT - 1, last, whole)
 
 
@@ -245,12 +244,13 @@
 
 
 def finish(acc, at, o_ref):
-    per = TILE // o_ref.shape[2]
-    width = o_ref.shape[2]
-    for t in range(o_ref.shape[1] // per):
+    _, size_x, size_y, width = o_ref.shape
+    per = TILE // width
+    for t in range(size_x * size_y // per):
         both = merged(acc[at + t])
         for j in range(per):
-            o_ref[:, t * per + j, :] = both[3:6, j * width : (j + 1) * width]
+            at_row = t * per + j
+            o_ref[:, at_row // size_y, at_row % size_y, :] = both[3:6, j * width : (j + 1) * width]
 
 
 def rest_kernel(axes, half, meta, live, mate_meta, x_both, table, sent_ref, o_ref, acc):
@@ -272,11 +272,11 @@
             lax.rem(lax.div(owner, counts[2]), counts[1]),
             lax.rem(owner, counts[2]),
         )
-        at = 0
+        at = ()
         for k in (2, 1, 0):
             shifts = axes[k][1]
             rel = lax.rem(owners[k] - here[k] + counts[k], counts[k])
-            at = at * len(shifts) + sum(jnp.where(rel == d, i, 0) for i, d in enumerate(shifts))
+            at = at + (sum(jnp.where(rel == d, i, 0) for i, d in enumerate(shifts)),)
         return at
 
     @pl.loop(0, lax.div(total + GROUP - 1, GROUP))
@@ -403,6 +403,11 @@
 
 
 ANY = pl.BlockSpec(memory_space=pl.ANY)
+HELD = pltpu.VMEM
+
+
+def held(*arrays):
+    return tuple(pltpu.with_memory_space_constraint(x, pltpu.VMEM) for x in arrays)
 
 
 def gather_call(axes, half, nodes, pos, coef, pairs, live):
@@ -412,13 +417,13 @@
     return pl.pallas_call(
         functools.partial(gather_kernel, axes, half),
         out_shape=(
-            jax.ShapeDtypeStruct((ntiles - LATE, 8, TILE), f32),
-            jax.ShapeDtypeStruct((spans[2], spans[1], spans[0], CT - 1, 8, TILE), f32),
-            jax.ShapeDtypeStruct((2,) + nodes.shape, f32),
+            HELD((ntiles - LATE, 8, TILE), f32),
+            HELD((spans[2], spans[1], spans[0], CT - 1, 8, TILE), f32),
+            HELD((2,) + nodes.shape, f32),
             jax.ShapeDtypeStruct((8, pairs.shape[1]), jnp.int32),
         ),
         in_specs=[SM, SM, VM, VM, VM, VM],
-        out_specs=(VM, ANY, ANY, ANY),
+        out_specs=(VM, VM, VM, ANY),
         scratch_shapes=[
             pltpu.VMEM((CT - 1, 8, TILE), f32),
             pltpu.VMEM((8, pairs.shape[1]), jnp.int32),
@@ -434,9 +439,9 @@
     )(pairs, live, nodes, pos, coef, pairs)
 
 
-def rest_call(axes, half, pairs, live, mate_meta, x_both, table):
+def rest_call(axes, half, pairs, live, mate_meta, x_both, table, block):
     ntiles = x_both.shape[2] * x_both.shape[3] // TILE
-    shape = jax.ShapeDtypeStruct(x_both.shape[1:], f32)
+    shape = HELD(block, f32)
     return pl.pallas_call(
         functools.partial(rest_kernel, axes, half),
         out_shape=(shape, shape),
@@ -444,7 +449,7 @@
         out_specs=(VM, VM),
         scratch_shapes=[pltpu.VMEM((2 * ntiles + 1, 16, TILE), f32)],
         name="rest",
-    )(pairs, live, mate_meta, x_both, table)
+    )(pairs, live, mate_meta, *held(x_both, table))
 
 
 def smooth_call(half, pairs, nodes, pos, coef, first, sent, mine, flags):
@@ -453,7 +458,7 @@
     lanes = min(128, size_z)
     return pl.pallas_call(
         functools.partial(smooth_kernel, half),
-        out_shape=jax.ShapeDtypeStruct(shape, f32),
+        out_shape=HELD(shape, f32),
         in_specs=[SM] + [VM] * 7,
         out_specs=VM,
         scratch_shapes=[
@@ -471,7 +476,24 @@
         ],
         compiler_params=pltpu.CompilerParams(collective_id=1, has_side_effects=True),
         name="smooth",
-    )(pairs, nodes, pos, coef, first, sent, mine, flags)
+    )(pairs, nodes, pos, coef, *held(first, sent, mine), flags)
+
+
+def store_kernel(x_ref, o_ref, sem):
+    copy = pltpu.make_async_copy(x_ref, o_ref, sem)
+    copy.start()
+    copy.wait()
+
+
+def store_call(moved):
+    return pl.pallas_call(
+        store_kernel,
+        out_shape=jax.ShapeDtypeStruct(moved.shape, f32),
+        in_specs=[VM],
+        out_specs=ANY,
+        scratch_shapes=[pltpu.SemaphoreType.DMA],
+        name="store",
+    )(*held(moved))
 
 
 def offsets(count, wanted):
@@ -503,13 +525,13 @@
     first, table, x_both, mate_meta = gather_call(
         axes, half, nodes, control_positions, control_coefficient_values, pairs, live_counts
     )
-    table = table.reshape((-1,) + table.shape[4:])
-    sent, mine = rest_call(axes, half, pairs, live_counts, mate_meta, x_both, table)
     shape = node_positions.shape
-    return smooth_call(
+    sent, mine = rest_call(axes, half, pairs, live_counts, mate_meta, x_both, table, shape)
+    moved = smooth_call(
         half, pairs, nodes, control_positions, control_coefficient_values, first,
-        sent.reshape(shape), mine.reshape(shape), sliver_flags,
+        sent, mine, sliver_flags,
     )
+    return store_call(moved)
 
 
 def solution(mesh):

time: 66.9 us -> 63.1 us (0.943)
  Pallas kernels: 64.4 us -> 62.1 us
  local copies, waits for them, and re-layouts: 1.62 us -> 0 us
    unnamed x1 -> x0, local copies, waits for them, and re-layouts: 1.62 us -> none
    pallas_call x1, Pallas kernels: 24.9 us -> 23.6 us  [rest_call(): pl.pallas_call(functools.partial(rest_kernel, axes, half), out_shape=(sha...]
    pallas_call x2 -> x3, Pallas kernels: 39.5 us -> 38.4 us  [the longest x1 19 us: gather_call(): pl.pallas_call(functools.partial(gather_kernel, axes, half), out_shape=(H...]
where the time goes in v4:
time: 63.1 us; the launch traced here: 62.9 us
  Pallas kernels  62.1 us (98%)
  between operations  0.83 us (1%)
    pallas_call x1, Pallas kernels, rest_call(): pl.pallas_call(functools.partial(rest_kernel, axes, half), out_shape=(sha...  23.6 us
    pallas_call x1, Pallas kernels, gather_call(): pl.pallas_call(functools.partial(gather_kernel, axes, half), out_shape=(H...  19 us
    pallas_call x1, Pallas kernels, smooth_call(): pl.pallas_call(functools.partial(smooth_kernel, half), out_shape=HELD(sha...  18.7 us

profile of v4, /device:TPU:0, one launch (start us, length us, event | category | flops | bytes accessed | tf_op | source)
XLA Modules:
  0.0 62.9 jit_solution(5996940701102202658)
XLA Ops:
  0.7 19.0 %gather.1 = (f32[20,8,512]{2,1,0:T(8,128)S(1)}, f32[2,3,4,3,8,512]{5,4,3,2,1,0:T(8,128)S(1)}, f32[2,3,64,256]{3,2,1,0:T(8,128)S(1)}, s32[8,128]{1,0:T(8,128)}) custom-call(s32[3,128]{1,0:T(4,128)} %bitcast.4, s32[1]{0:T(128)S(6)} %copy.7.live_ref.live, f32[3,64,256]{2,1,0:T(8,128)} %bitcast.2, f32[3,2048]{1,0:T(4,128)} %pos_ref.3, f32[3,2048]{1,0:T(4,128)} %coef_ref.3, ...), custom_call_target="tpu_custom_call" | custom-call | tf_op jit(solution)/shard_map/gather/pallas_call | solution.py:417
  19.7 23.6 %rest.1 = (f32[3,8,8,256]{3,2,1,0:T(8,128)S(1)}, f32[3,8,8,256]{3,2,1,0:T(8,128)S(1)}) custom-call(s32[3,128]{1,0:T(4,128)} %bitcast.6, s32[1]{0:T(128)S(6)} %copy.7.live_ref.live, s32[8,128]{1,0:T(8,128)} %get-tuple-element.12.mate_meta, f32[2,3,64,256]{3,2,1,0:T(8,128)S(1)} %get-tuple-element.13.x_both, f32[2,3,4,3,8,512]{5,4,3,2,1,0:T(8,128)S(1)} %get-tuple-element.14.table), custom_call_target="tpu_custom_call" | custom-call | tf_op jit(solution)/shard_map/rest/pallas_call | solution.py:445
  43.3 18.7 %smooth.1.x_ref = f32[3,8,8,256]{3,2,1,0:T(8,128)S(1)} custom-call(s32[3,128]{1,0:T(4,128)} %bitcast.7, f32[3,64,256]{2,1,0:T(8,128)} %bitcast.3, f32[3,2048]{1,0:T(4,128)} %pos_ref.3, f32[3,2048]{1,0:T(4,128)} %coef_ref.3, f32[20,8,512]{2,1,0:T(8,128)S(1)} %get-tuple-element.11.first_ref, f32[3,8,8,256]{3,2,1,0:T(8,128)S(1)} %get-tuple-element.15.sent_ref, ...), custom_call_target="tpu_custom_call" | custom-call | tf_op jit(solution)/shard_map/smooth/pallas_call | solution.py:459
  62.0 0.7 %store.1 = f32[3,8,8,256]{3,2,1,0:T(8,128)} custom-call(f32[3,8,8,256]{3,2,1,0:T(8,128)S(1)} %smooth.1.x_ref), custom_call_target="tpu_custom_call" | custom-call | tf_op jit(solution)/shard_map/store/pallas_call | solution.py:489
